TPU v7x, 32 devices: a whole 2x2x4 slice. The times are simulated.
32 devices in a mesh: parts: 2 (over x), blk: 16 (over z, y, core).
Axes of the slice: x: 2, y: 2, z: 4, core: 2. Of those that a mesh axis runs over, the one named last changes fastest.
Arguments:
- queries: bfloat16 [2048, 4096], P(('parts', 'blk')), parts along dimension 0, may hold values from -12 to 12
- keys: bfloat16 [2048, 512], P(('parts', 'blk')), parts along dimension 0, may hold values from -12 to 12
- values: bfloat16 [2048, 512], P(('parts', 'blk')), parts along dimension 0, may hold values from -6 to 6
- span_order: int32 [64], P('parts'), parts along dimension 0, may hold values from 0 to 31, as said below
Outputs:
- attended: bfloat16 [2048, 4096], P(('parts', 'blk')), parts along dimension 0
There are 2 independent parts, one for each index of `parts`. A program takes and returns all parts, laid end to end along the dimension named above; each array names one. Nothing has to cross between parts.
Inputs may be any that keep to these rules, and one draw needn't show every extreme that they name: `span_order`: a permutation of the 32 blocks; slots 2i and 2i+1 hold blocks c and 31 - c for some c.
All inputs are finite; a program needn't handle non-finite values.
Results may differ from a plain program's by a relative error of at most 0.0065.
Values may be sent and summed in bfloat16 or wider, within the bound.
A program may use at most 64 MiB of HBM per device.

v0:
```python
import jax
import jax.numpy as jnp
from jax import lax
from jax.sharding import PartitionSpec as P

HEAD = 128


def from_partner(value, axis, bit):
    return lax.ppermute(value, axis, [(i, i ^ 1 << bit) for i in range(lax.axis_size(axis))])


def passed_along(value, axis, by):
    count = lax.axis_size(axis)
    return lax.ppermute(value, axis, [(i, (i + by) % count) for i in range(count)])


def attend(state, query_rows, query_pos, key_rows, value_rows, key_pos, scale):
    running, total, summed = state
    scores = (
        jnp.einsum("rkgd,ckd->kgrc", query_rows, key_rows, preferred_element_type=jnp.float32)
        * scale
    )
    scores = jnp.where(
        key_pos[None, None, None, :] <= query_pos[None, None, :, None], scores, -jnp.inf
    )
    newest = jnp.maximum(running, jnp.max(scores, axis=-1))
    factor = jnp.exp(running - newest)
    expo = jnp.exp(scores - newest[..., None])
    total = total * factor + jnp.sum(expo, axis=-1)
    weights = expo.astype(jnp.bfloat16)
    summed = summed * factor[..., None] + jnp.einsum(
        "kgrc,ckd->kgrd", weights, value_rows, preferred_element_type=jnp.float32
    )
    return (newest, total, summed)


def block_width(count, unit):
    number = count // unit
    best = 1
    for divisor in range(1, number + 1):
        if number % divisor == 0 and divisor * unit <= 1024:
            best = divisor
    return best * unit


def sweep(state, query_rows, query_pos, key_rows, value_rows, key_pos, scale, width):
    count = key_rows.shape[0]
    blocks = count // width
    stacked = (
        key_rows.reshape((blocks, width) + key_rows.shape[1:]),
        value_rows.reshape((blocks, width) + value_rows.shape[1:]),
        key_pos.reshape(blocks, width),
    )

    def step(carry, item):
        return (attend(carry, query_rows, query_pos, item[0], item[1], item[2], scale), None)

    final, unused = lax.scan(step, state, stacked)
    return final


def fresh(kv_heads, group, count):
    return (
        jnp.full((kv_heads, group, count), -1e30, jnp.float32),
        jnp.zeros((kv_heads, group, count), jnp.float32),
        jnp.zeros((kv_heads, group, count, HEAD), jnp.float32),
    )


def butterfly(data, member, width_bits, trade):
    current = data[:, None]
    for bit in range(width_bits):
        mine = member // 2**bit % 2
        shaped = current.reshape((current.shape[0] // 2, 2) + current.shape[1:])
        keep = lax.dynamic_index_in_dim(shaped, mine, 1, keepdims=False)
        send = lax.dynamic_index_in_dim(shaped, 1 - mine, 1, keepdims=False)
        got = trade(send, bit)
        lower = jnp.where(mine == 0, keep, got)
        upper = jnp.where(mine == 0, got, keep)
        joined = jnp.stack([lower, upper], axis=1)
        current = joined.reshape(
            (joined.shape[0], joined.shape[1] * joined.shape[2]) + joined.shape[3:]
        )
    return current[0]


def per_device(queries, keys, values, span_order):
    rows = queries.shape[0]
    span = rows // 2
    kv_heads = keys.shape[1] // HEAD
    group = queries.shape[1] // (kv_heads * HEAD)
    scale = 1.0 / HEAD**0.5
    width_bits = kv_heads.bit_length() - 1
    member = lax.axis_index("blk") % kv_heads
    group_index = lax.axis_index("blk") // kv_heads
    cycle = lax.axis_size("blk") // kv_heads
    group_rows = kv_heads * rows
    q_parts = queries.reshape(rows, kv_heads, group * HEAD).transpose(1, 0, 2)
    k_parts = keys.reshape(rows, kv_heads, HEAD).transpose(1, 0, 2)
    v_parts = values.reshape(rows, kv_heads, HEAD).transpose(1, 0, 2)
    packed = jnp.concatenate([q_parts, k_parts, v_parts], axis=2)

    def trade_in(item, bit):
        return from_partner(item, "blk", bit)

    regrouped = butterfly(packed, member, width_bits, trade_in).reshape(
        group_rows, group * HEAD + 2 * HEAD
    )
    q_mine = regrouped[:, : group * HEAD].reshape(group_rows, 1, group, HEAD)
    kv_buffer = regrouped[:, group * HEAD :]
    index = group_index * group_rows + jnp.arange(group_rows, dtype=jnp.int32)
    query_pos = span_order[index // span] * span + index % span
    steps = cycle.bit_length() - 1
    for level in range(steps):
        arrived = passed_along(kv_buffer, "blk", kv_heads * 2**level)
        kv_buffer = jnp.concatenate([arrived, kv_buffer], axis=0)
    count = kv_buffer.shape[0]
    index = ((group_index + 1) * group_rows + jnp.arange(count, dtype=jnp.int32)) % count
    key_pos = span_order[index // span] * span + index % span
    key_rows = kv_buffer[:, :HEAD].reshape(count, 1, HEAD)
    value_rows = kv_buffer[:, HEAD:].reshape(count, 1, HEAD)
    width = block_width(count, group_rows)
    running, total, summed = sweep(
        fresh(1, group, group_rows), q_mine, query_pos, key_rows, value_rows, key_pos, scale, width
    )
    normed = (summed / total[..., None]).astype(jnp.bfloat16)
    result_rows = normed[0].transpose(1, 0, 2).reshape(kv_heads, rows, group * HEAD)

    def trade_out(item, bit):
        return from_partner(item, "blk", bit)

    returned = butterfly(result_rows, member, width_bits, trade_out)
    return returned.transpose(1, 0, 2).reshape(rows, kv_heads * group * HEAD)


def solution(mesh):
    return jax.shard_map(
        per_device,
        mesh=mesh,
        in_specs=(
            P(("parts", "blk"), None),
            P(("parts", "blk"), None),
            P(("parts", "blk"), None),
            P("parts"),
        ),
        out_specs=P(("parts", "blk"), None),
        check_vma=False,
    )
```

profile of v0, /device:TPU:0, one launch (start us, length us, event | category | flops | bytes accessed | tf_op | source)
XLA Modules:
  0.0 76.9 jit_solution(9296775565707114232)
XLA Ops:
  0.0 0.9 %reshape.291 = bf16[64,4,128]{2,1,0:T(4,128)(2,1)S(1)} reshape(bf16[64,512]{1,0:T(8,128)(2,1)} %param.5) | data formatting | bytes 131072 | tf_op jit(solution)/shard_map/reshape | solution.py:100
  0.9 0.9 %reshape.292 = bf16[64,4,128]{2,1,0:T(4,128)(2,1)S(1)} reshape(bf16[64,512]{1,0:T(8,128)(2,1)} %param.6) | data formatting | bytes 131072 | tf_op jit(solution)/shard_map/reshape | solution.py:101
  1.7 1.4 %reshape.290 = bf16[64,4,1024]{2,1,0:T(4,128)(2,1)S(1)} reshape(bf16[64,4096]{1,0:T(8,128)(2,1)} %param.4) | data formatting | bytes 1048576 | tf_op jit(solution)/shard_map/reshape | solution.py:99
  3.2 0.3 pad_maximum_fusion
  3.5 0.2 reshape_broadcast_in_dim.3
  3.8 1.4 %constant_dynamic-slice_fusion.1 = (bf16[2,1,1,64,1280]{4,1,0,3,2:T(2,128)(2,1)S(1)}, bf16[2,1,1,64,1280]{4,1,0,3,2:T(2,128)(2,1)S(1)}) fusion(bf16[2,2,1,64,1280]{4,1,0,3,2:T(2,128)(2,1)S(1)} %reshape_broadcast_in_dim.3, s32[]{:T(128)S(6)} %select_n.192, s32[]{:T(128)S(6)} %select_n.193), kind=kLoop, calls=%fused_computation.140 | loop fusion | bytes 1310728 | tf_op jit(solution)/shard_map/jit(dynamic_index_in_dim)/dynamic_slice | solution.py:76
  5.2 0.6 collective-permute-start
  5.7 0.1 compare_reduce_fusion.24
  5.8 0.1 compare_reduce_fusion.22
  5.9 0.1 compare_reduce_fusion.18
  5.9 0.1 compare_reduce_fusion.20
  6.0 0.1 compare_reduce_fusion.16
  6.1 0.1 compare_reduce_fusion.14
  6.2 0.1 compare_reduce_fusion.12
  6.2 0.1 compare_reduce_fusion.6
  6.3 0.1 compare_reduce_fusion.10
  6.4 0.1 compare_reduce_fusion.2
  6.5 0.1 compare_reduce_fusion.8
  6.5 0.1 compare_reduce_fusion.4
  6.6 0.1 compare_reduce_fusion
  6.7 0.3 collective-permute-done
  7.0 0.1 fusion.20
  7.1 2.9 %collective-permute-start.1 = (bf16[1,2,64,1280]{3,2,1,0:T(8,128)(2,1)S(1)}, bf16[1,2,64,1280]{3,2,1,0:T(8,128)(2,1)S(1)}, u32[]{:S(2)}, u32[]{:S(2)}) collective-permute-start(bf16[1,2,64,1280]{3,2,1,0:T(8,128)(2,1)S(1)} %fusion.16), channel_id=1, source_target_pairs={{0,2},{1,3},{2,0},{3,1},{4,6},{5,7},{6,4},{7,5},{8,10},{9,11},{10,... | collective-permute-start | bytes 983048 | tf_op jit(solution)/shard_map/ppermute | solution.py:10
  10.0 0.7 fusion.40
  10.8 4.3 %compare_select_fusion.3 = s32[1024,1]{0,1:T(1,128)S(1)} fusion(s32[]{:T(128)} %bitcast.25, s32[]{:T(128)} %bitcast.26, s32[]{:T(128)} %bitcast.27, s32[]{:T(128)} %bitcast.28, s32[]{:T(128)} %bitcast.29, s32[]{:T(128)} %bitcast.31, s32[]{:T(128)} %bitcast.30, s32[]{:T(128)S(6)} %mul.55), kind=kLoop, calls=%fused_computation.78 | loop fusion | flops 43008 | bytes 4128 | tf_op jit(solution)/shard_map/gather | solution.py:120
  15.1 0.7 fusion.39
  15.8 2.2 %collective-permute-done.1 = bf16[1,2,64,1280]{3,2,1,0:T(8,128)(2,1)S(1)} collective-permute-done((bf16[1,2,64,1280]{3,2,1,0:T(8,128)(2,1)S(1)}, bf16[1,2,64,1280]{3,2,1,0:T(8,128)(2,1)S(1)}, u32[]{:S(2)}, u32[]{:S(2)}) %collective-permute-start.1) | collective-permute-done | bytes 327712 | tf_op jit(solution)/shard_map/ppermute | solution.py:10
  18.1 0.1 pad_maximum_fusion.1
  18.2 1.8 %collective-permute-start.2 = (bf16[256,256]{1,0:T(8,128)(2,1)S(1)}, bf16[256,256]{1,0:T(8,128)(2,1)S(1)}, u32[]{:S(2)}, u32[]{:S(2)}) collective-permute-start(bf16[256,256]{1,0:T(8,128)(2,1)S(1)} %slice.82), channel_id=1, source_target_pairs={{0,4},{1,5},{2,6},{3,7},{4,8},{5,9},{6,10},{7,11},{8,12},{9,13},{1... | collective-permute-start | bytes 393224 | tf_op jit(solution)/shard_map/ppermute | solution.py:15
  20.0 15.8 %fusion.30 = s32[1024]{0:T(1024)S(1)} fusion(pred[1024]{0:T(1024)(128)(4,1)S(1)} %get-tuple-element.78, pred[1024]{0:T(1024)(128)(4,1)S(1)} %get-tuple-element.79, pred[1024]{0:T(1024)(128)(4,1)S(1)} %get-tuple-element.80, pred[1024]{0:T(1024)(128)(4,1)S(1)} %get-tuple-element.81, pred[1024]{0:T(1024)(128)(4,1)S(1)} %get-tuple-element.82, ...), kind=kLoop, calls=%fused_computation.100 | loop fusion | flops 51200 | bytes 33896 | tf_op jit(solution)/shard_map/add | solution.py:120
  36.3 4.3 %compare_select_fusion.13 = s32[256,1]{0,1:T(1,128)S(1)} fusion(s32[]{:T(128)} %bitcast.25, s32[]{:T(128)} %bitcast.26, s32[]{:T(128)} %bitcast.27, s32[]{:T(128)} %bitcast.28, s32[]{:T(128)} %bitcast.29, s32[]{:T(128)} %bitcast.31, s32[]{:T(128)} %bitcast.30, s32[]{:T(128)S(6)} %mul.57), kind=kLoop, calls=%fused_computation.132 | loop fusion | flops 7936 | bytes 1056 | tf_op jit(solution)/shard_map/gather | solution.py:113
  40.6 2.7 %collective-permute-start.3 = (bf16[512,256]{1,0:T(8,128)(2,1)S(1)}, bf16[512,256]{1,0:T(8,128)(2,1)S(1)}, u32[]{:S(2)}, u32[]{:S(2)}) collective-permute-start(bf16[512,256]{1,0:T(8,128)(2,1)S(1)} %pad_maximum_fusion.4), channel_id=1, source_target_pairs={{0,8},{1,9},{2,10},{3,11},{4,12},{5,13},{6,14},{7,15},{8,0},{9,1},... | collective-permute-start | bytes 786440 | tf_op jit(solution)/shard_map/ppermute | solution.py:15
  43.3 15.8 %fusion.35 = s32[256]{0:T(256)S(1)} fusion(pred[256]{0:T(512)(128)(4,1)S(1)} %get-tuple-element.102, pred[256]{0:T(512)(128)(4,1)S(1)} %get-tuple-element.103, pred[256]{0:T(512)(128)(4,1)S(1)} %get-tuple-element.104, pred[256]{0:T(512)(128)(4,1)S(1)} %get-tuple-element.105, pred[256]{0:T(512)(128)(4,1)S(1)} %get-tuple-element.106, ...), kind=kLoop, calls=%fused_computation.147 | loop fusion | flops 9984 | bytes 8552 | tf_op jit(solution)/shard_map/add | solution.py:113
  59.1 0.2 broadcast_compare_fusion
  59.3 0.1 slice.84
  59.3 0.2 copy.28
  59.6 0.0 collective-permute-done.3
  59.6 1.3 %fusion.2 = (f32[8,256]{1,0:T(8,128)S(1)}, f32[1024,256,8]{1,0,2:T(8,128)S(1)}) fusion(pred[256,1024]{0,1:T(8,128)(4,1)S(1)} %broadcast_compare_fusion, bf16[256,8,128]{0,2,1:T(8,128)(2,1)S(1)} %bitcast.152, bf16[1024,256]{1,0:T(8,128)(2,1)S(1)} %pad_maximum_fusion.2), kind=kOutput, calls=%fused_computation.4 | convolution fusion | flops 543160320 | bytes 9445376 | tf_op jit(solution)/shard_map/while/body/eval_jaxpr/rkgd,ckd->kgrc/dot_general | solution.py:21
  61.0 1.7 %fusion = f32[8,256]{1,0:T(8,128)S(1)} fusion(f32[1024,256,8]{1,0,2:T(8,128)S(1)} %get-tuple-element.77, f32[8,256]{1,0:T(8,128)S(1)} %get-tuple-element.43, pred[256,1024]{0,1:T(8,128)(4,1)S(1)} %broadcast_compare_fusion), kind=kLoop, calls=%fused_computation.2 | loop fusion | flops 8386560 | bytes 8667136 | tf_op jit(solution)/shard_map/while/body/eval_jaxpr/reduce_sum | solution.py:30
  62.7 2.5 %divide_convert_fusion = bf16[256,8,128]{2,0,1:T(8,128)(2,1)S(1)} fusion(f32[1024,256,8]{1,0,2:T(8,128)S(1)} %get-tuple-element.77, f32[8,256]{1,0:T(8,128)S(1)} %get-tuple-element.43, pred[256,1024]{0,1:T(8,128)(4,1)S(1)} %broadcast_compare_fusion, f32[256,8]{0,1:T(8,128)S(1)} %bitcast_add_fusion, f32[256,8]{0,1:T(8,128)S(1)} %get-tuple-element.42, ...), kind=kOutput, calls=%fused_computation.10 | convolution fusion | flops 546045952 | bytes 9461760 | tf_op jit(solution)/shard_map/while/body/eval_jaxpr/kgrc,ckd->kgrd/dot_general | solution.py:32
  65.2 0.3 copy.31
  65.6 0.2 reshape_broadcast_in_dim_reshape.3
  65.9 0.1 collective-permute-start.4
  65.9 1.5 %collective-permute-done.4 = bf16[2,1,64,1024]{3,2,0,1:T(8,128)(2,1)S(1)} collective-permute-done((bf16[2,1,64,1024]{3,2,0,1:T(8,128)(2,1)S(1)}, bf16[2,1,64,1024]{3,2,0,1:T(8,128)(2,1)S(1)}, u32[]{:S(2)}, u32[]{:S(2)}) %collective-permute-start.4) | collective-permute-done | bytes 262176 | tf_op jit(solution)/shard_map/ppermute | solution.py:10
  67.5 1.6 %collective-permute-start.5 = (bf16[1,2,64,1024]{3,2,1,0:T(8,128)(2,1)S(1)}, bf16[1,2,64,1024]{3,2,1,0:T(8,128)(2,1)S(1)}, u32[]{:S(2)}, u32[]{:S(2)}) collective-permute-start(bf16[1,2,64,1024]{3,2,1,0:T(8,128)(2,1)S(1)} %fusion.22), channel_id=1, source_target_pairs={{0,2},{1,3},{2,0},{3,1},{4,6},{5,7},{6,4},{7,5},{8,10},{9,11},{10,... | collective-permute-start | bytes 786440 | tf_op jit(solution)/shard_map/ppermute | solution.py:10
  69.1 6.8 %collective-permute-done.5 = bf16[1,2,64,1024]{3,2,1,0:T(8,128)(2,1)S(1)} collective-permute-done((bf16[1,2,64,1024]{3,2,1,0:T(8,128)(2,1)S(1)}, bf16[1,2,64,1024]{3,2,1,0:T(8,128)(2,1)S(1)}, u32[]{:S(2)}, u32[]{:S(2)}) %collective-permute-start.5) | collective-permute-done | bytes 262176 | tf_op jit(solution)/shard_map/ppermute | solution.py:10
  76.0 0.1 pad_maximum_fusion.3
  76.1 0.8 %copy.35 = bf16[4,8,8,1024]{3,2,0,1:T(8,128)(2,1)} copy(bf16[4,8,8,1024]{3,2,1,0:T(8,128)(2,1)S(1)} %bitcast.151) | data formatting | bytes 1048576 | tf_op jit(solution)/shard_map/reshape | solution.py:134
  (28 shorter events, 0.8 us)
Async XLA Ops:
  0.0 10.0 %copy-start = (s32[32]{0:T(128)S(1)}, s32[32]{0:T(128)}, u32[]{:S(2)}) copy-start(s32[32]{0:T(128)} %param.7) | copy-start | bytes 388
  5.2 1.8 %collective-permute-start = (bf16[2,1,64,1280]{3,2,0,1:T(8,128)(2,1)S(1)}, bf16[2,1,64,1280]{3,2,0,1:T(8,128)(2,1)S(1)}, u32[]{:S(2)}, u32[]{:S(2)}) collective-permute-start(bf16[2,1,64,1280]{3,2,0,1:T(8,128)(2,1)S(1)} %bitcast.153), channel_id=1, source_target_pairs={{0,1},{1,0},{2,3},{3,2},{4,5},{5,4},{6,7},{7,6},{8,9},{9,8},{10,11... | collective-permute-start | bytes 983048 | tf_op jit(solution)/shard_map/ppermute | solution.py:10
  7.1 11.0 %collective-permute-start.1 = (bf16[1,2,64,1280]{3,2,1,0:T(8,128)(2,1)S(1)}, bf16[1,2,64,1280]{3,2,1,0:T(8,128)(2,1)S(1)}, u32[]{:S(2)}, u32[]{:S(2)}) collective-permute-start(bf16[1,2,64,1280]{3,2,1,0:T(8,128)(2,1)S(1)} %fusion.16), channel_id=1, source_target_pairs={{0,2},{1,3},{2,0},{3,1},{4,6},{5,7},{6,4},{7,5},{8,10},{9,11},{10,... | collective-permute-start | bytes 983048 | tf_op jit(solution)/shard_map/ppermute | solution.py:10
  18.2 22.4 %collective-permute-start.2 = (bf16[256,256]{1,0:T(8,128)(2,1)S(1)}, bf16[256,256]{1,0:T(8,128)(2,1)S(1)}, u32[]{:S(2)}, u32[]{:S(2)}) collective-permute-start(bf16[256,256]{1,0:T(8,128)(2,1)S(1)} %slice.82), channel_id=1, source_target_pairs={{0,4},{1,5},{2,6},{3,7},{4,8},{5,9},{6,10},{7,11},{8,12},{9,13},{1... | collective-permute-start | bytes 393224 | tf_op jit(solution)/shard_map/ppermute | solution.py:15
  40.6 18.9 %collective-permute-start.3 = (bf16[512,256]{1,0:T(8,128)(2,1)S(1)}, bf16[512,256]{1,0:T(8,128)(2,1)S(1)}, u32[]{:S(2)}, u32[]{:S(2)}) collective-permute-start(bf16[512,256]{1,0:T(8,128)(2,1)S(1)} %pad_maximum_fusion.4), channel_id=1, source_target_pairs={{0,8},{1,9},{2,10},{3,11},{4,12},{5,13},{6,14},{7,15},{8,0},{9,1},... | collective-permute-start | bytes 786440 | tf_op jit(solution)/shard_map/ppermute | solution.py:15
  65.9 1.6 %collective-permute-start.4 = (bf16[2,1,64,1024]{3,2,0,1:T(8,128)(2,1)S(1)}, bf16[2,1,64,1024]{3,2,0,1:T(8,128)(2,1)S(1)}, u32[]{:S(2)}, u32[]{:S(2)}) collective-permute-start(bf16[2,1,64,1024]{3,2,0,1:T(8,128)(2,1)S(1)} %dynamic-slice_bitcast_fusion), channel_id=1, source_target_pairs={{0,1},{1,0},{2,3},{3,2},{4,5},{5,4},{6,7},{7,6},{8,9},{9,8},{10,11... | collective-permute-start | bytes 786440 | tf_op jit(solution)/shard_map/ppermute | solution.py:10
  67.5 8.4 %collective-permute-start.5 = (bf16[1,2,64,1024]{3,2,1,0:T(8,128)(2,1)S(1)}, bf16[1,2,64,1024]{3,2,1,0:T(8,128)(2,1)S(1)}, u32[]{:S(2)}, u32[]{:S(2)}) collective-permute-start(bf16[1,2,64,1024]{3,2,1,0:T(8,128)(2,1)S(1)} %fusion.22), channel_id=1, source_target_pairs={{0,2},{1,3},{2,0},{3,1},{4,6},{5,7},{6,4},{7,5},{8,10},{9,11},{10,... | collective-permute-start | bytes 786440 | tf_op jit(solution)/shard_map/ppermute | solution.py:10
where the time goes:
time: 77.7 us; the launch traced here: 76.9 us
  other arithmetic  44.3 us (57%)
  waiting for transfers between devices  10.9 us (14%)
  starting transfers between devices  9.66 us (12%)
  local copies, waits for them, and re-layouts  7.95 us (10%)
  matrix products  3.86 us (5%)
    add x1, other arithmetic, per_device(): key_pos = span_order[index // span] * span + index % span  15.8 us
    add x1, other arithmetic, per_device(): query_pos = span_order[index // span] * span + index % span  15.8 us
    ppermute x4, waiting for transfers between devices, from_partner(): lax.ppermute(value, axis, [(i, i ^ 1 << bit) for i in range(lax.axis_size...  10.9 us
    gather x14, other arithmetic, per_device(): key_pos = span_order[index // span] * span + index % span  5.29 us
    ppermute x4, starting transfers between devices, from_partner(): lax.ppermute(value, axis, [(i, i ^ 1 << bit) for i in range(lax.axis_size...  5.16 us
    gather x14, other arithmetic, per_device(): query_pos = span_order[index // span] * span + index % span  4.73 us
    ppermute x2, starting transfers between devices, passed_along(): lax.ppermute(value, axis, [(i, (i + by) % count) for i in range(count)])  4.5 us
    dot_general x1, matrix products, attend(): jnp.einsum('kgrc,ckd->kgrd', weights, value_rows, preferred_element_type=...  2.51 us
  transfers between devices with their start and end apart: 6, of which 4 were waited for; matrix products, arithmetic and copies ran while one was open for 57% of the time, Pallas kernels for 0%

commit v1 on v0

--- a/solution.py
+++ b/solution.py
@@ -1,6 +1,10 @@
+import functools
+
 import jax
 import jax.numpy as jnp
 from jax import lax
+from jax.experimental import pallas as pl
+from jax.experimental.pallas import tpu as pltpu
 from jax.sharding import PartitionSpec as P
 
 HEAD = 128
@@ -134,9 +138,247 @@
     return returned.transpose(1, 0, 2).reshape(rows, kv_heads * group * HEAD)
 
 
+MASKED = -1e30
+LOG2E = 1.4426950408889634
+MESH = pl.DeviceIdType.MESH
+SEMAPHORES = 512
+
+
+def units_of(groups):
+    far = groups // 2
+    found = []
+    for distance in range(1, far + 1):
+        for side in (-1, 1):
+            half = None if distance < far else (0 if side < 0 else 1)
+            found.append((distance, side, half))
+    return found
+
+
+def fused_kernel(
+    n, order_ref, q_hbm, k_hbm, v_hbm, out_hbm,
+    kv, q_ref, bias, out_ref, local_sem, send_sem, recv_sem,
+):
+    rows = q_hbm.shape[0]
+    span = rows // 2
+    kv_heads = kv.shape[0]
+    tokens = kv.shape[1]
+    group = q_hbm.shape[1] // (kv_heads * HEAD)
+    groups = n // 4
+    me = lax.axis_index("blk")
+    base = me - me % 4
+    core = me % 2
+    side_bit = me // 2 % 2
+    sib = base + 2 * side_bit + (1 - core)
+    partner = base + 2 * (1 - side_bit) + core
+    cross = base + 2 * (1 - side_bit) + (1 - core)
+    ring = {1: (me + 4) % n, -1: (me + n - 4) % n}
+    units = units_of(groups)
+    far = groups // 2
+
+    local = []
+
+    def local_copy(src, dst):
+        copy = pltpu.make_async_copy(src, dst, local_sem.at[len(local)])
+        copy.start()
+        local.append(copy)
+        return copy
+
+    own_rows = pl.ds(pl.multiple_of(me * rows, rows), rows)
+    fills = []
+    for k in range(kv_heads):
+        columns = pl.ds(k * HEAD, HEAD)
+        fills.append(
+            (
+                local_copy(k_hbm.at[:, columns], kv.at[k, own_rows, pl.ds(0, HEAD)]),
+                local_copy(v_hbm.at[:, columns], kv.at[k, own_rows, pl.ds(HEAD, HEAD)]),
+            )
+        )
+    q_copy = local_copy(q_hbm, q_ref)
+
+    barrier = pltpu.get_barrier_semaphore()
+    for other in (sib, partner, ring[1], ring[-1]):
+        pl.semaphore_signal(barrier, inc=1, device_id={"blk": other}, device_id_type=MESH)
+
+    q_span = [order_ref[2 * me], order_ref[2 * me + 1]]
+    row = lax.broadcasted_iota(jnp.int32, (rows, 128), 0)
+    lane = lax.broadcasted_iota(jnp.int32, (rows, 128), 1)
+    q_pos = jnp.where(row < span, q_span[0], q_span[1]) * span + row % span
+    per_tile = 128 // span
+    for tile in range(tokens // 128):
+        held = jnp.full((rows, 128), order_ref[tile * per_tile], jnp.int32)
+        for i in range(1, per_tile):
+            held = jnp.where(lane >= i * span, order_ref[tile * per_tile + i], held)
+        k_pos = held * span + lane % span
+        bias[:, tile * 128 : (tile + 1) * 128] = jnp.where(k_pos <= q_pos, 0.0, MASKED)
+
+    pl.semaphore_wait(barrier, 4)
+
+    sent = []
+
+    def piece(k, slot, half):
+        if half is None:
+            return kv.at[k, pl.ds(pl.multiple_of(slot * rows, rows), rows)]
+        return kv.at[k, pl.ds(pl.multiple_of(slot * rows + half * span, span), span)]
+
+    def remote(k, slot, half, to, send):
+        ref = piece(k, slot, half)
+        return pltpu.make_async_remote_copy(
+            src_ref=ref,
+            dst_ref=ref,
+            send_sem=send,
+            recv_sem=recv_sem.at[k, slot, half or 0],
+            device_id={"blk": to},
+            device_id_type=MESH,
+        )
+
+    def send(k, slot, half, to):
+        copy = remote(k, slot, half, to, send_sem.at[len(sent)])
+        copy.start()
+        sent.append(copy)
+
+    def arrive(k, slot, half):
+        remote(k, slot, half, sib, send_sem.at[0]).wait_recv()
+
+    def slot_at(origin, distance, side):
+        return (origin + n + side * 4 * distance) % n
+
+    def start_ring(k, origin):
+        for side in (-1, 1):
+            half = None if far > 1 else (0 if side < 0 else 1)
+            send(k, origin, half, ring[-side])
+
+    def own(k):
+        for fill in fills[k]:
+            fill.wait()
+        send(k, me, None, partner)
+        start_ring(k, me)
+        send(k, me, None, sib)
+
+    def along(k, origin, distance, side, half, to_partner):
+        slot = slot_at(origin, distance, side)
+        arrive(k, slot, half)
+        if distance < far:
+            ahead = None if distance + 1 < far else (0 if side < 0 else 1)
+            send(k, slot, ahead, ring[-side])
+        if to_partner:
+            send(k, slot, half, partner)
+        send(k, slot, half, sib)
+
+    def by_partner(k):
+        return k % 2 == 0
+
+    def relay(k):
+        for distance, side, half in units:
+            if distance == 1:
+                along(k, me, distance, side, half, by_partner(k))
+        arrive(k, partner, None)
+        if not by_partner(k):
+            start_ring(k, partner)
+        send(k, partner, None, sib)
+        for distance, side, half in units:
+            if distance > 1:
+                along(k, me, distance, side, half, by_partner(k))
+        for distance, side, half in units:
+            if by_partner(k):
+                slot = slot_at(partner, distance, side)
+                arrive(k, slot, half)
+                send(k, slot, half, sib)
+            else:
+                along(k, partner, distance, side, half, False)
+
+    def gathered(k):
+        for origin in (sib, cross):
+            arrive(k, origin, None)
+            for distance, side, half in units:
+                arrive(k, slot_at(origin, distance, side), half)
+
+    factor = LOG2E / HEAD**0.5
+    stacked = min(group, 4)
+    written = []
+
+    def compute(k):
+        keys = kv[k, :, :HEAD]
+        values = kv[k, :, HEAD:]
+        for part in range(group // stacked):
+            first = k * group + part * stacked
+            q = jnp.concatenate(
+                [q_ref[:, (first + j) * HEAD : (first + j + 1) * HEAD] for j in range(stacked)],
+                axis=0,
+            )
+            scores = lax.dot_general(
+                q, keys, (((1,), (1,)), ((), ())), preferred_element_type=jnp.float32
+            )
+            scores = scores.reshape(stacked, rows, tokens) * factor + bias[...][None]
+            top = jnp.max(scores, axis=-1, keepdims=True)
+            expo = jnp.exp2(scores - top)
+            total = jnp.sum(expo, axis=-1, keepdims=True)
+            weights = expo.astype(jnp.bfloat16).reshape(stacked * rows, tokens)
+            summed = jnp.dot(weights, values, preferred_element_type=jnp.float32)
+            normed = (summed.reshape(stacked, rows, HEAD) / total).astype(jnp.bfloat16)
+            for j in range(stacked):
+                out_ref[:, (first + j) * HEAD : (first + j + 1) * HEAD] = normed[j]
+        columns = pl.ds(k * group * HEAD, group * HEAD)
+        written.append(local_copy(out_ref.at[:, columns], out_hbm.at[:, columns]))
+
+    own(0)
+    if kv_heads > 1:
+        own(1)
+    for k in range(kv_heads + 1):
+        if k < kv_heads:
+            relay(k)
+            if k + 2 < kv_heads:
+                own(k + 2)
+        if k == 1:
+            q_copy.wait()
+        if k > 0:
+            gathered(k - 1)
+            compute(k - 1)
+    for copy in sent:
+        copy.wait_send()
+    for copy in written:
+        copy.wait()
+
+
+def semaphores_sent(kv_heads, groups):
+    count = len(units_of(groups))
+    return kv_heads * (5 + 2 + 3 * count + count + 4)
+
+
+def fused(n, queries, keys, values, span_order):
+    rows = queries.shape[0]
+    kv_heads = keys.shape[1] // HEAD
+    tokens = n * rows
+    anywhere = pl.BlockSpec(memory_space=pl.ANY)
+    return pl.pallas_call(
+        functools.partial(fused_kernel, n),
+        out_shape=jax.ShapeDtypeStruct(queries.shape, jnp.bfloat16),
+        in_specs=[pl.BlockSpec(memory_space=pltpu.SMEM), anywhere, anywhere, anywhere],
+        out_specs=anywhere,
+        scratch_shapes=[
+            pltpu.VMEM((kv_heads, tokens, 2 * HEAD), jnp.bfloat16),
+            pltpu.VMEM(queries.shape, jnp.bfloat16),
+            pltpu.VMEM((rows, tokens), jnp.float32),
+            pltpu.VMEM(queries.shape, jnp.bfloat16),
+            pltpu.SemaphoreType.DMA((3 * kv_heads + 1,)),
+            pltpu.SemaphoreType.DMA((semaphores_sent(kv_heads, n // 4),)),
+            pltpu.SemaphoreType.DMA((kv_heads, n, 2)),
+        ],
+        compiler_params=pltpu.CompilerParams(collective_id=0, has_side_effects=True),
+    )(span_order, queries, keys, values)
+
+
 def solution(mesh):
+    n = mesh.shape["blk"]
+
+    def step(queries, keys, values, span_order):
+        kv_heads = keys.shape[1] // HEAD
+        needed = kv_heads * n * 2 + semaphores_sent(kv_heads, n // 4)
+        if n % 8 == 0 and needed <= SEMAPHORES:
+            return fused(n, queries, keys, values, span_order)
+        return per_device(queries, keys, values, span_order)
+
     return jax.shard_map(
-        per_device,
+        step,
         mesh=mesh,
         in_specs=(
             P(("parts", "blk"), None),

time: 77.7 us -> 48.2 us (0.62)
  Pallas kernels: 0 us -> 46.2 us
  other arithmetic: 44.3 us -> 0 us
  waiting for transfers between devices: 10.9 us -> 0 us
  starting transfers between devices: 9.66 us -> 0 us
  local copies, waits for them, and re-layouts: 7.95 us -> 1.87 us
  matrix products: 3.86 us -> 0 us
    pallas_call x0 -> x1, Pallas kernels: none -> 46.2 us  [fused(): pl.pallas_call(functools.partial(fused_kernel, n), out_shape=jax.ShapeDty...]
    add x3 -> x0, other arithmetic: 31.6 us -> none  [the longest x1 15.8 us: per_device(): key_pos = span_order[index // span] * span + index % span]
    ppermute x6 -> x0, waiting for transfers between devices: 10.9 us -> none  [the longest x4 10.9 us: from_partner(): lax.ppermute(value, axis, [(i, i ^ 1 << bit) for i in range(lax.axis_size...]
    gather x28 -> x0, other arithmetic: 10 us -> none  [the longest x14 5.29 us: per_device(): key_pos = span_order[index // span] * span + index % span]
    ppermute x6 -> x0, starting transfers between devices: 9.66 us -> none  [the longest x4 5.16 us: from_partner(): lax.ppermute(value, axis, [(i, i ^ 1 << bit) for i in range(lax.axis_size...]
    reshape x4 -> x0, local copies, waits for them, and re-layouts: 4 us -> none  [the longest x1 1.43 us: per_device(): q_parts = queries.reshape(rows, kv_heads, group * HEAD).transpose(1, 0, 2)]
    dot_general x2 -> x0, matrix products: 3.86 us -> none  [the longest x1 2.51 us: attend(): jnp.einsum('kgrc,ckd->kgrd', weights, value_rows, preferred_element_type=...]
    unnamed x2 -> x1, local copies, waits for them, and re-layouts: 0.01 us -> 1.87 us
  transfers between devices with their start and end apart: 6 -> 0, of which waited for: 4 -> 0; matrix products, arithmetic and copies ran while one was open for 57% -> 0% of each run, Pallas kernels for 0% -> 0%
where the time goes in v1:
time: 48.2 us; the launch traced here: 48.1 us
  Pallas kernels  46.2 us (96%)
  local copies, waits for them, and re-layouts  1.87 us (4%)
    pallas_call x1, Pallas kernels, fused(): pl.pallas_call(functools.partial(fused_kernel, n), out_shape=jax.ShapeDty...  46.2 us
    unnamed x1, local copies, waits for them, and re-layouts  1.87 us

profile of v1, /device:TPU:0, one launch (start us, length us, event | category | flops | bytes accessed | tf_op | source)
XLA Modules:
  0.0 48.1 jit_solution(12954580249130435291)
XLA Ops:
  0.0 46.2 %shard_map.46 = bf16[64,4096]{1,0:T(8,128)(2,1)} custom-call(s32[32]{0:T(128)} %order_ref.1, bf16[64,4096]{1,0:T(8,128)(2,1)} %q_hbm.1, bf16[64,512]{1,0:T(8,128)(2,1)} %k_hbm.1, bf16[64,512]{1,0:T(8,128)(2,1)} %v_hbm.1), custom_call_target="tpu_custom_call" | custom-call | tf_op jit(solution)/shard_map/pallas_call | solution.py:352
  46.2 1.9 %copy.6 = bf16[64,4096]{1,0:T(8,128)(2,1)} copy(bf16[64,4096]{1,0:T(8,128)(2,1)} %shard_map.46) | data formatting | bytes 1048576

commit v2 on v0

--- a/solution.py
+++ b/solution.py
@@ -1,6 +1,10 @@
+import functools
+
 import jax
 import jax.numpy as jnp
 from jax import lax
+from jax.experimental import pallas as pl
+from jax.experimental.pallas import tpu as pltpu
 from jax.sharding import PartitionSpec as P
 
 HEAD = 128
@@ -134,9 +138,236 @@
     return returned.transpose(1, 0, 2).reshape(rows, kv_heads * group * HEAD)
 
 
+MASKED = -1e30
+LOG2E = 1.4426950408889634
+MESH = pl.DeviceIdType.MESH
+SEMAPHORES = 512
+CHUNKS = 2
+
+
+def fused_kernel(
+    n, order_ref, q_hbm, k_hbm, v_hbm, out_hbm,
+    kv, q_ref, bias, out_ref, local_sem, send_sem, recv_sem,
+):
+    rows = q_hbm.shape[0]
+    span = rows // 2
+    kv_heads = k_hbm.shape[1] // HEAD
+    chunks = kv.shape[0]
+    per_chunk = kv_heads // chunks
+    tokens = kv.shape[1]
+    group = q_hbm.shape[1] // (kv_heads * HEAD)
+    me = lax.axis_index("blk")
+    base = me - me % 4
+    core = me % 2
+    side_bit = me // 2 % 2
+    sib = base + 2 * side_bit + (1 - core)
+    partner = base + 2 * (1 - side_bit) + core
+    cross = base + 2 * (1 - side_bit) + (1 - core)
+    groups = n // 4
+    place = me // 4
+    mirrored = place * 2 // groups
+    relayed = groups > 3
+    edge = jnp.logical_or(place == 0, place == groups - 1)
+    inner = jnp.logical_or(place == 1, place == groups - 2)
+    beside_edge = (me + 4 * (1 - 2 * (1 - mirrored)) + n) % n
+
+    def along(origin, distance):
+        return (origin + 4 * (distance + mirrored * (groups - 2 * distance))) % n
+
+    distances = list(range(1, groups))
+    local = []
+
+    def local_copy(src, dst):
+        copy = pltpu.make_async_copy(src, dst, local_sem.at[len(local)])
+        copy.start()
+        local.append(copy)
+        return copy
+
+    own_rows = pl.ds(pl.multiple_of(me * rows, rows), rows)
+    fills = []
+    wide = per_chunk * HEAD
+    for k in range(chunks):
+        columns = pl.ds(k * wide, wide)
+        fills.append(
+            (
+                local_copy(k_hbm.at[:, columns], kv.at[k, own_rows, pl.ds(0, wide)]),
+                local_copy(v_hbm.at[:, columns], kv.at[k, own_rows, pl.ds(wide, wide)]),
+            )
+        )
+    q_copy = local_copy(q_hbm, q_ref)
+
+    barrier = pltpu.get_barrier_semaphore()
+    others = [sib, partner] + [along(me, d) for d in distances]
+    for other in others:
+        pl.semaphore_signal(barrier, inc=1, device_id={"blk": other}, device_id_type=MESH)
+
+    q_span = [order_ref[2 * me], order_ref[2 * me + 1]]
+    row = lax.broadcasted_iota(jnp.int32, (rows, 128), 0)
+    lane = lax.broadcasted_iota(jnp.int32, (rows, 128), 1)
+    q_pos = jnp.where(row < span, q_span[0], q_span[1]) * span + row % span
+    per_tile = 128 // span
+    for tile in range(tokens // 128):
+        held = jnp.full((rows, 128), order_ref[tile * per_tile], jnp.int32)
+        for i in range(1, per_tile):
+            held = jnp.where(lane >= i * span, order_ref[tile * per_tile + i], held)
+        k_pos = held * span + lane % span
+        bias[:, tile * 128 : (tile + 1) * 128] = jnp.where(k_pos <= q_pos, 0.0, MASKED)
+
+    pl.semaphore_wait(barrier, len(others))
+
+    sent = []
+
+    def remote(k, slot, to, send):
+        ref = kv.at[k, pl.ds(pl.multiple_of(slot * rows, rows), rows)]
+        return pltpu.make_async_remote_copy(
+            src_ref=ref,
+            dst_ref=ref,
+            send_sem=send,
+            recv_sem=recv_sem.at[k, slot],
+            device_id={"blk": to},
+            device_id_type=MESH,
+        )
+
+    def send(k, slot, to, when=None):
+        copy = remote(k, slot, to, send_sem.at[len(sent)])
+        sent.append((copy, when))
+        if when is None:
+            copy.start()
+        else:
+            pl.when(when)(copy.start)
+
+    def arrive(k, slot):
+        remote(k, slot, sib, send_sem.at[0]).wait_recv()
+
+    def own(k):
+        for fill in fills[k]:
+            fill.wait()
+        for d in sorted(distances, key=lambda d: d != groups - 2):
+            when = jnp.logical_not(edge) if relayed and d == groups - 1 else None
+            send(k, me, along(me, d), when)
+        send(k, me, sib)
+
+    def own_across(k):
+        send(k, me, partner)
+
+    def line(k):
+        for d in sorted(distances, key=lambda d: (d == groups - 1, d)):
+            slot = along(me, d)
+            arrive(k, slot)
+            if relayed and d == groups - 2:
+                send(k, slot, beside_edge, inner)
+            send(k, slot, partner)
+            send(k, slot, sib)
+
+    def across(k):
+        for slot in [partner] + [along(partner, d) for d in distances]:
+            arrive(k, slot)
+            send(k, slot, sib)
+
+    def gathered(k):
+        for origin in (sib, cross):
+            for slot in [origin] + [along(origin, d) for d in distances]:
+                arrive(k, slot)
+
+    factor = LOG2E / HEAD**0.5
+    stacked = min(group, 4)
+    written = []
+
+    def compute(k, part):
+        at = k % per_chunk * HEAD
+        keys = kv[k // per_chunk, :, at : at + HEAD]
+        values = kv[k // per_chunk, :, wide + at : wide + at + HEAD]
+        first = k * group + part * stacked
+        q = jnp.concatenate(
+            [q_ref[:, (first + j) * HEAD : (first + j + 1) * HEAD] for j in range(stacked)],
+            axis=0,
+        )
+        scores = lax.dot_general(
+            q, keys, (((1,), (1,)), ((), ())), preferred_element_type=jnp.float32
+        )
+        scores = scores.reshape(stacked, rows, tokens) * factor + bias[...][None]
+        top = jnp.max(scores, axis=-1, keepdims=True)
+        expo = jnp.exp2(scores - top)
+        total = jnp.sum(expo, axis=-1, keepdims=True)
+        weights = expo.astype(jnp.bfloat16).reshape(stacked * rows, tokens)
+        summed = jnp.dot(weights, values, preferred_element_type=jnp.float32)
+        normed = (summed.reshape(stacked, rows, HEAD) / total).astype(jnp.bfloat16)
+        for j in range(stacked):
+            out_ref[:, (first + j) * HEAD : (first + j + 1) * HEAD] = normed[j]
+        if part == parts - 1:
+            columns = pl.ds(k * group * HEAD, group * HEAD)
+            written.append(local_copy(out_ref.at[:, columns], out_hbm.at[:, columns]))
+
+    parts = group // stacked
+    slots = {}
+    bodies = per_chunk * parts
+    for k in range(chunks):
+        slots.setdefault(3 * k, []).append((line, k))
+        slots.setdefault(3 * k + 4, []).append((across, k))
+        slots.setdefault(3 * k + 6, []).append((gathered, k))
+        for body in range(bodies):
+            slots.setdefault(3 * k + 6 + 3 * body / bodies, []).append(
+                (compute, k * per_chunk + body // parts, body % parts)
+            )
+    for k in range(chunks):
+        own(k)
+        if k < 2:
+            own_across(k)
+    q_copy.wait()
+    for time in sorted(slots):
+        for action in slots[time]:
+            action[0](*action[1:])
+            if action[0] is line and action[1] + 2 < chunks:
+                own_across(action[1] + 2)
+    for copy, when in sent:
+        if when is None:
+            copy.wait_send()
+        else:
+            pl.when(when)(copy.wait_send)
+    for copy in written:
+        copy.wait()
+
+
+def semaphores_sent(kv_heads, groups):
+    return kv_heads * (5 * groups + 2)
+
+
+def fused(n, queries, keys, values, span_order):
+    rows = queries.shape[0]
+    kv_heads = keys.shape[1] // HEAD
+    tokens = n * rows
+    chunks = CHUNKS if kv_heads % CHUNKS == 0 else 1
+    anywhere = pl.BlockSpec(memory_space=pl.ANY)
+    return pl.pallas_call(
+        functools.partial(fused_kernel, n),
+        out_shape=jax.ShapeDtypeStruct(queries.shape, jnp.bfloat16),
+        in_specs=[pl.BlockSpec(memory_space=pltpu.SMEM), anywhere, anywhere, anywhere],
+        out_specs=anywhere,
+        scratch_shapes=[
+            pltpu.VMEM((chunks, tokens, kv_heads // chunks * 2 * HEAD), jnp.bfloat16),
+            pltpu.VMEM(queries.shape, jnp.bfloat16),
+            pltpu.VMEM((rows, tokens), jnp.float32),
+            pltpu.VMEM(queries.shape, jnp.bfloat16),
+            pltpu.SemaphoreType.DMA((3 * kv_heads + 1,)),
+            pltpu.SemaphoreType.DMA((semaphores_sent(kv_heads, n // 4),)),
+            pltpu.SemaphoreType.DMA((chunks, n)),
+        ],
+        compiler_params=pltpu.CompilerParams(collective_id=0, has_side_effects=True),
+    )(span_order, queries, keys, values)
+
+
 def solution(mesh):
+    n = mesh.shape["blk"]
+
+    def step(queries, keys, values, span_order):
+        kv_heads = keys.shape[1] // HEAD
+        needed = kv_heads * n + semaphores_sent(kv_heads, n // 4)
+        if n % 8 == 0 and needed <= SEMAPHORES:
+            return fused(n, queries, keys, values, span_order)
+        return per_device(queries, keys, values, span_order)
+
     return jax.shard_map(
-        per_device,
+        step,
         mesh=mesh,
         in_specs=(
             P(("parts", "blk"), None),

time: 77.7 us -> 29.6 us (0.38)
  other arithmetic: 44.3 us -> 0 us
  Pallas kernels: 0 us -> 27.6 us
  waiting for transfers between devices: 10.9 us -> 0 us
  starting transfers between devices: 9.66 us -> 0 us
  local copies, waits for them, and re-layouts: 7.95 us -> 1.87 us
  matrix products: 3.86 us -> 0 us
    add x3 -> x0, other arithmetic: 31.6 us -> none  [the longest x1 15.8 us: per_device(): key_pos = span_order[index // span] * span + index % span]
    pallas_call x0 -> x1, Pallas kernels: none -> 27.6 us  [fused(): pl.pallas_call(functools.partial(fused_kernel, n), out_shape=jax.ShapeDty...]
    ppermute x6 -> x0, waiting for transfers between devices: 10.9 us -> none  [the longest x4 10.9 us: from_partner(): lax.ppermute(value, axis, [(i, i ^ 1 << bit) for i in range(lax.axis_size...]
    gather x28 -> x0, other arithmetic: 10 us -> none  [the longest x14 5.29 us: per_device(): key_pos = span_order[index // span] * span + index % span]
    ppermute x6 -> x0, starting transfers between devices: 9.66 us -> none  [the longest x4 5.16 us: from_partner(): lax.ppermute(value, axis, [(i, i ^ 1 << bit) for i in range(lax.axis_size...]
    reshape x4 -> x0, local copies, waits for them, and re-layouts: 4 us -> none  [the longest x1 1.43 us: per_device(): q_parts = queries.reshape(rows, kv_heads, group * HEAD).transpose(1, 0, 2)]
    dot_general x2 -> x0, matrix products: 3.86 us -> none  [the longest x1 2.51 us: attend(): jnp.einsum('kgrc,ckd->kgrd', weights, value_rows, preferred_element_type=...]
    unnamed x2 -> x1, local copies, waits for them, and re-layouts: 0.01 us -> 1.87 us
  transfers between devices with their start and end apart: 6 -> 0, of which waited for: 4 -> 0; matrix products, arithmetic and copies ran while one was open for 57% -> 0% of each run, Pallas kernels for 0% -> 0%
where the time goes in v2:
time: 29.6 us; the launch traced here: 29.5 us
  Pallas kernels  27.6 us (93%)
  local copies, waits for them, and re-layouts  1.87 us (6%)
    pallas_call x1, Pallas kernels, fused(): pl.pallas_call(functools.partial(fused_kernel, n), out_shape=jax.ShapeDty...  27.6 us
    unnamed x1, local copies, waits for them, and re-layouts  1.87 us

profile of v2, /device:TPU:0, one launch (start us, length us, event | category | flops | bytes accessed | tf_op | source)
XLA Modules:
  0.0 29.5 jit_solution(4253895580915795442)
XLA Ops:
  0.0 27.6 %shard_map.46 = bf16[64,4096]{1,0:T(8,128)(2,1)} custom-call(s32[32]{0:T(128)} %order_ref.1, bf16[64,4096]{1,0:T(8,128)(2,1)} %q_hbm.1, bf16[64,512]{1,0:T(8,128)(2,1)} %k_hbm.1, bf16[64,512]{1,0:T(8,128)(2,1)} %v_hbm.1), custom_call_target="tpu_custom_call" | custom-call | tf_op jit(solution)/shard_map/pallas_call | solution.py:341
  27.6 1.9 %copy.6 = bf16[64,4096]{1,0:T(8,128)(2,1)} copy(bf16[64,4096]{1,0:T(8,128)(2,1)} %shard_map.46) | data formatting | bytes 1048576

commit v3 on v2

--- a/solution.py
+++ b/solution.py
@@ -143,11 +143,12 @@
 MESH = pl.DeviceIdType.MESH
 SEMAPHORES = 512
 CHUNKS = 2
+LINE = 4
 
 
 def fused_kernel(
     n, order_ref, q_hbm, k_hbm, v_hbm, out_hbm,
-    kv, q_ref, bias, out_ref, local_sem, send_sem, recv_sem,
+    kv, q_ref, bias, out_ref, local_sem, send_sem, recv_sem, told,
 ):
     rows = q_hbm.shape[0]
     span = rows // 2
@@ -167,7 +168,6 @@
     place = me // 4
     mirrored = place * 2 // groups
     relayed = groups > 3
-    edge = jnp.logical_or(place == 0, place == groups - 1)
     inner = jnp.logical_or(place == 1, place == groups - 2)
     beside_edge = (me + 4 * (1 - 2 * (1 - mirrored)) + n) % n
 
@@ -197,9 +197,14 @@
     q_copy = local_copy(q_hbm, q_ref)
 
     barrier = pltpu.get_barrier_semaphore()
-    others = [sib, partner] + [along(me, d) for d in distances]
-    for other in others:
-        pl.semaphore_signal(barrier, inc=1, device_id={"blk": other}, device_id_type=MESH)
+    def greet(semaphore, other):
+        pl.semaphore_signal(semaphore, inc=1, device_id={"blk": other}, device_id_type=MESH)
+
+    last = groups - 1
+    for other in (sib, partner, along(me, 1)):
+        greet(barrier, other)
+    if relayed:
+        pl.when(inner)(functools.partial(greet, barrier, along(me, last)))
 
     q_span = [order_ref[2 * me], order_ref[2 * me + 1]]
     row = lax.broadcasted_iota(jnp.int32, (rows, 128), 0)
@@ -213,7 +218,20 @@
         k_pos = held * span + lane % span
         bias[:, tile * 128 : (tile + 1) * 128] = jnp.where(k_pos <= q_pos, 0.0, MASKED)
 
-    pl.semaphore_wait(barrier, len(others))
+    if relayed:
+
+        @pl.when(inner)
+        def tell():
+            pl.semaphore_wait(barrier, 4)
+            greet(told, along(me, 1))
+            greet(told, along(me, last))
+
+        @pl.when(jnp.logical_not(inner))
+        def listen():
+            pl.semaphore_wait(barrier, 3)
+
+    else:
+        pl.semaphore_wait(barrier, 3)
 
     sent = []
 
@@ -242,8 +260,12 @@
     def own(k):
         for fill in fills[k]:
             fill.wait()
-        for d in sorted(distances, key=lambda d: d != groups - 2):
-            when = jnp.logical_not(edge) if relayed and d == groups - 1 else None
+        if k == 0:
+            own_across(0)
+        for d in sorted(distances, key=lambda d: (d == groups - 2) == (k == 0)):
+            if relayed and k == 0 and d == groups - 2:
+                pl.semaphore_wait(told, 1)
+            when = inner if relayed and d == last else None
             send(k, me, along(me, d), when)
         send(k, me, sib)
 
@@ -251,7 +273,7 @@
         send(k, me, partner)
 
     def line(k):
-        for d in sorted(distances, key=lambda d: (d == groups - 1, d)):
+        for d in sorted(distances, key=lambda d: (d == groups - 1, d != groups - 2, d)):
             slot = along(me, d)
             arrive(k, slot)
             if relayed and d == groups - 2:
@@ -311,7 +333,7 @@
             )
     for k in range(chunks):
         own(k)
-        if k < 2:
+        if k == 1:
             own_across(k)
     q_copy.wait()
     for time in sorted(slots):
@@ -351,6 +373,7 @@
             pltpu.SemaphoreType.DMA((3 * kv_heads + 1,)),
             pltpu.SemaphoreType.DMA((semaphores_sent(kv_heads, n // 4),)),
             pltpu.SemaphoreType.DMA((chunks, n)),
+            pltpu.SemaphoreType.REGULAR,
         ],
         compiler_params=pltpu.CompilerParams(collective_id=0, has_side_effects=True),
     )(span_order, queries, keys, values)
@@ -362,7 +385,7 @@
     def step(queries, keys, values, span_order):
         kv_heads = keys.shape[1] // HEAD
         needed = kv_heads * n + semaphores_sent(kv_heads, n // 4)
-        if n % 8 == 0 and needed <= SEMAPHORES:
+        if n % 8 == 0 and n // 4 <= LINE and needed <= SEMAPHORES:
             return fused(n, queries, keys, values, span_order)
         return per_device(queries, keys, values, span_order)
 

time: 29.6 us -> 28.8 us (0.973)
  Pallas kernels: 27.6 us -> 26.8 us
    pallas_call x1, Pallas kernels: 27.6 us -> 26.8 us  [fused(): pl.pallas_call(functools.partial(fused_kernel, n), out_shape=jax.ShapeDty...]
where the time goes in v3:
time: 28.8 us; the launch traced here: 28.6 us
  Pallas kernels  26.8 us (93%)
  local copies, waits for them, and re-layouts  1.87 us (6%)
    pallas_call x1, Pallas kernels, fused(): pl.pallas_call(functools.partial(fused_kernel, n), out_shape=jax.ShapeDty...  26.8 us
    unnamed x1, local copies, waits for them, and re-layouts  1.87 us

profile of v3, /device:TPU:0, one launch (start us, length us, event | category | flops | bytes accessed | tf_op | source)
XLA Modules:
  0.0 28.6 jit_solution(11258912111270382931)
XLA Ops:
  0.0 26.8 %shard_map.46 = bf16[64,4096]{1,0:T(8,128)(2,1)} custom-call(s32[32]{0:T(128)} %order_ref.1, bf16[64,4096]{1,0:T(8,128)(2,1)} %q_hbm.1, bf16[64,512]{1,0:T(8,128)(2,1)} %k_hbm.1, bf16[64,512]{1,0:T(8,128)(2,1)} %v_hbm.1), custom_call_target="tpu_custom_call" | custom-call | tf_op jit(solution)/shard_map/pallas_call | solution.py:363
  26.8 1.9 %copy.6 = bf16[64,4096]{1,0:T(8,128)(2,1)} copy(bf16[64,4096]{1,0:T(8,128)(2,1)} %shard_map.46) | data formatting | bytes 1048576
